TPU v7x, 32 devices: a whole 2x2x4 slice. The times are simulated.
32 devices in a mesh: row: 4 (over x, core), col: 8 (over z, y).
Axes of the slice: x: 2, y: 2, z: 4, core: 2. Of those that a mesh axis runs over, the one named last changes fastest.
Arguments:
- eigenvectors: float32 [2048, 1024], P('row', 'col'), may hold values from -6 to 6
- householder: float32 [3, 8, 512, 256], P(None, 'row', None, 'col'), may hold values from -6 to 6
Outputs:
- transformed: float32 [2048, 1024], P('row', 'col')
All inputs are finite; a program needn't handle non-finite values.
Results may differ from a plain program's by a relative error of at most 0.0003.
Values sent between devices are 32-bit elements; how exact they have to be, the bound alone decides.
A program may use at most 192 MiB of HBM per device.

v0:
```python
import jax
import jax.numpy as jnp
from jax import lax
from jax.sharding import PartitionSpec as P

REFL = 256


PRECISE = lax.Precision.HIGHEST


def prefix_2(part, axis, combine, identity):
    place = lax.axis_index(axis)
    gathered = jax.tree.map(lambda a: lax.all_gather(a, axis), part)
    state = jax.tree.map(lambda a, e: jnp.zeros_like(a) + jnp.asarray(e, a.dtype), part, identity)

    def one(hop, state):
        return combine(
            state, jax.tree.map(lambda a: lax.dynamic_index_in_dim(a, hop, 0, False), gathered)
        )

    return lax.fori_loop(0, place, one, state)


def shifted(value, axis, steps):
    count = lax.axis_size(axis)
    initial, last = (max(0, -steps), min(count, count - steps))
    return lax.ppermute(value, axis, [(source, source + steps) for source in range(initial, last)])


def inner_product(left, right):
    return lax.dot_general(
        left, right, (((0,), (0,)), ((), ())), precision=PRECISE, preferred_element_type=jnp.float32
    )


def product(left, right):
    return jnp.dot(left, right, precision=PRECISE, preferred_element_type=jnp.float32)


def invert_upper(upper):
    order = upper.shape[0]
    rows_idx = lax.broadcasted_iota(jnp.int32, (order, order), 0)
    cols_idx = lax.broadcasted_iota(jnp.int32, (order, order), 1)
    inverse = jnp.where(rows_idx == cols_idx, 1.0 / jnp.diagonal(upper)[:, None], jnp.float32(0.0))
    size = 1
    while size < order:
        inside_old = rows_idx // size == cols_idx // size
        inside_new = rows_idx // (2 * size) == cols_idx // (2 * size)
        corners = jnp.where(inside_new & jnp.logical_not(inside_old), upper, jnp.float32(0.0))
        inverse = inverse - product(product(inverse, corners), inverse)
        size = 2 * size
    return inverse


def block_inverse(vectors):
    gram_matrix = inner_product(vectors, vectors)
    upper_part = jnp.triu(gram_matrix, 1) + jnp.diag(jnp.diagonal(gram_matrix) * 0.5)
    return invert_upper(upper_part)


def reflect(stripe, vectors, inverse):
    weights = inner_product(vectors, stripe)
    scaled = product(inverse, weights)
    return stripe - product(vectors, scaled)


def compose(earlier, later):
    return (product(later[0], earlier[0]), product(later[0], earlier[1]) + later[1])


def apply_owner(extended, vectors, inverses, per_device, is_first):
    width = vectors.shape[2]
    pieces = []
    held = extended[:width]
    for block_index in range(per_device):
        first_row = (block_index + 1) * width
        stripe = jnp.concatenate([held, extended[first_row : first_row + width]], axis=0)
        updated = reflect(stripe, vectors[block_index], inverses[block_index])
        if block_index == 0:
            updated = jnp.where(is_first, stripe, updated)
        pieces.append(updated[:width])
        held = updated[width:]
    pieces.append(held)
    return jnp.concatenate(pieces, axis=0)


def shards(eigenvectors, householder):
    sweeps_total = householder.shape[0]
    per_device = householder.shape[1]
    devices_row = lax.axis_size("row")
    position = lax.axis_index("row")
    is_first = position == 0
    is_last = position == devices_row - 1
    row_count = eigenvectors.shape[0]
    columns = eigenvectors.shape[1]
    gathered = lax.all_gather(householder, "col", axis=3, tiled=True)
    inverses_all = jax.vmap(jax.vmap(block_inverse))(gathered)
    matrix = eigenvectors
    for sweep_index in range(sweeps_total):
        current = gathered[sweep_index]
        inverses = inverses_all[sweep_index]
        top_rows = jnp.concatenate(
            [jnp.zeros((REFL, columns), jnp.float32), jnp.eye(REFL, dtype=jnp.float32)], axis=1
        )
        lower_rows = jnp.concatenate([matrix, jnp.zeros((row_count, REFL), jnp.float32)], axis=1)
        extended = apply_owner(
            jnp.concatenate([top_rows, lower_rows], axis=0), current, inverses, per_device, is_first
        )
        tail_const = extended[row_count:, :columns]
        tail_map = extended[row_count:, columns:]
        identity = (jnp.eye(REFL, dtype=jnp.float32), jnp.zeros((REFL, columns), jnp.float32))
        prefix = prefix_2((tail_map, tail_const), "row", compose, identity)
        incoming = prefix[1]
        result = extended[:, :columns] + product(extended[:, columns:], incoming)
        handed = shifted(result[:REFL], "row", -1)
        own_rows = result[REFL:]
        matrix = jnp.concatenate(
            [
                own_rows[: row_count - REFL],
                jnp.where(is_last, own_rows[row_count - REFL :], handed),
            ],
            axis=0,
        )
    return matrix


def solution(mesh):
    in_specs = (P("row", "col"), P(None, "row", None, "col"))
    out_specs = P("row", "col")
    return jax.shard_map(shards, mesh=mesh, in_specs=in_specs, out_specs=out_specs, check_vma=False)
```

profile of v0, /device:TPU:1, one launch (start us, length us, event | category | flops | bytes accessed | tf_op | source)
XLA Modules:
  0.0 329.5 jit_solution(12909376014592202942)
XLA Ops:
  17.6 52.3 %all-gather.11.cloned.1.call-done = f32[3,2,512,256]{2,3,1,0:T(8,128)} async-done(((f32[3,2,512,32]{2,3,1,0:T(8,128)}), f32[3,2,512,256]{2,3,1,0:T(8,128)}) %all-gather.11.cloned.1.call-update) | async-done | bytes 3145744 | tf_op jit(solution)/shard_map/all_gather | solution.py:97
  69.9 5.9 %fusion.106 = f32[3,2,256,256]{3,2,1,0:T(8,128)S(1)} fusion(f32[3,2,512,256]{2,3,1,0:T(8,128)} %all-gather.11.cloned.1.call-done), kind=kOutput, calls=%fused_computation.210 | convolution fusion | flops 2415919104 | bytes 4718592 | tf_op jit(solution)/shard_map/vmap(vmap())/dot_general | solution.py:32
  75.8 43.8 %copy.25 = f32[3,2,256,256]{0,1,3,2:T(2,128)} copy(f32[3,2,256,256]{3,2,1,0:T(8,128)S(1)} %fusion.106) | data formatting | bytes 3145728 | tf_op jit(solution)/shard_map/vmap(vmap())/dot_general | solution.py:32
  119.6 2.5 gather_fusion
  123.5 44.3 %copy.27 = f32[3,2,256,256]{0,1,3,2:T(2,128)} copy(f32[3,2,256,256]{3,2,1,0:T(8,128)S(1)} %select_add_fusion) | data formatting | bytes 3145728 | tf_op jit(solution)/shard_map/vmap(vmap())/add | solution.py:58
  167.9 2.5 gather_fusion.1
  170.6 1.8 fusion.11
  172.5 2.0 select_subtract_fusion
  179.6 1.9 convolution_subtract_fusion.5
  191.9 2.0 fusion.17
  207.2 9.9 %all-gather.1 = f32[1024,128]{0,1:T(8,128)} all-gather(f32[256,128]{0,1:T(8,128)S(1)} %slice.245), channel_id=3, replica_groups=mesh['row'=4,'col'=8] {'row'}, dimensions={0}, use_global_device_ids=true | all-gather | bytes 655360 | tf_op jit(solution)/shard_map/all_gather | solution.py:14
  217.1 2.1 copy.51
  219.2 4.8 %all-gather.13.cloned.1.call-done = f32[1024,256]{0,1:T(8,128)} async-done(((f32[256,256]{0,1:T(8,128)}), f32[1024,256]{0,1:T(8,128)}) %all-gather.13.cloned.1.call-update) | async-done | bytes 1048592 | tf_op jit(solution)/shard_map/all_gather | solution.py:14
  223.9 2.6 copy.50
  227.2 3.3 %while.36 = (s32[]{:T(128)}, f32[256,128]{1,0:T(8,128)}, s32[]{:T(128)}, f32[4,256,256]{2,1,0:T(8,128)}, f32[4,256,128]{2,1,0:T(8,128)}, /*index=5*/s32[]{:T(128)}, s32[]{:T(128)}, s32[]{:T(128)}) while((s32[]{:T(128)}, f32[256,128]{1,0:T(8,128)}, s32[]{:T(128)}, f32[4,256,256]{2,1,0:T(8,128)}, f32[4,256,128]{2,1,0:T(8,128)}, ...), condition=%wide.region_1.2_spmd, body=%wide.region_0.1_spmd.sunk | while | flops 100696064 | bytes 918647 | solution.py:22
  228.1 2.0 convolution_add_fusion.9
  230.5 1.9 convolution_add_fusion.5
  233.8 1.9 collective-permute-start
  235.7 6.1 %collective-permute-done = f32[256,128]{0,1:T(8,128)} collective-permute-done((f32[256,128]{0,1:T(8,128)}, f32[256,128]{0,1:T(8,128)}, u32[]{:S(2)}, u32[]{:S(2)}) %collective-permute-start) | collective-permute-done | bytes 131104 | tf_op jit(solution)/shard_map/ppermute | solution.py:28
  253.7 7.0 %all-gather.3 = f32[1024,128]{0,1:T(8,128)} all-gather(f32[256,128]{0,1:T(8,128)S(1)} %slice.258), channel_id=5, replica_groups=mesh['row'=4,'col'=8] {'row'}, dimensions={0}, use_global_device_ids=true | all-gather | bytes 655360 | tf_op jit(solution)/shard_map/all_gather | solution.py:14
  260.7 2.1 copy.53
  262.8 7.3 %all-gather.15.cloned.1.call-done = f32[1024,256]{0,1:T(8,128)} async-done(((f32[256,256]{0,1:T(8,128)}), f32[1024,256]{0,1:T(8,128)}) %all-gather.15.cloned.1.call-update) | async-done | bytes 1048592 | tf_op jit(solution)/shard_map/all_gather | solution.py:14
  270.1 2.6 copy.52
  273.3 2.9 while.37
  274.2 2.0 convolution_add_fusion.10
  276.2 1.9 convolution_add_fusion.4
  278.1 2.1 collective-permute-start.1
  280.2 5.6 %collective-permute-done.1 = f32[256,128]{0,1:T(8,128)S(1)} collective-permute-done((f32[256,128]{0,1:T(8,128)S(1)}, f32[256,128]{0,1:T(8,128)S(1)}, u32[]{:S(2)}, u32[]{:S(2)}) %collective-permute-start.1) | collective-permute-done | bytes 131104 | tf_op jit(solution)/shard_map/ppermute | solution.py:28
  295.8 6.6 %all-gather.5 = f32[1024,128]{0,1:T(8,128)S(1)} all-gather(f32[256,128]{0,1:T(8,128)S(1)} %slice.271), channel_id=7, replica_groups=mesh['row'=4,'col'=8] {'row'}, dimensions={0}, use_global_device_ids=true | all-gather | bytes 655360 | tf_op jit(solution)/shard_map/all_gather | solution.py:14
  302.6 9.6 %all-gather.17.cloned.1.call-done = f32[1024,256]{0,1:T(8,128)} async-done(((f32[256,256]{0,1:T(8,128)}), f32[1024,256]{0,1:T(8,128)}) %all-gather.17.cloned.1.call-update) | async-done | bytes 1048592 | tf_op jit(solution)/shard_map/all_gather | solution.py:14
  315.6 2.2 collective-permute-start.2
  317.8 4.1 %collective-permute-done.2 = f32[256,128]{0,1:T(8,128)S(1)} collective-permute-done((f32[256,128]{0,1:T(8,128)S(1)}, f32[256,128]{0,1:T(8,128)S(1)}, u32[]{:S(2)}, u32[]{:S(2)}) %collective-permute-start.2) | collective-permute-done | bytes 131104 | tf_op jit(solution)/shard_map/ppermute | solution.py:28
  (145 shorter events, 72.3 us)
Async XLA Ops:
  6.5 9.3 %copy-start.19 = (f32[512,128]{1,0:T(8,128)S(1)}, f32[512,128]{1,0:T(8,128)}, u32[]{:S(2)}) copy-start(f32[512,128]{1,0:T(8,128)} %param.8) | copy-start | bytes 786436
  6.5 63.3 %all-gather.11.cloned.1.call-start = ((), (), s32[]{:S(2)}) async-start(), calls=%async_computation | async-start | bytes 3538944 | tf_op jit(solution)/shard_map/all_gather | solution.py:97
  7.3 216.7 %all-gather.13.cloned.1.call-start = ((), (), s32[]{:S(2)}) async-start(), calls=%async_computation.1 | async-start | bytes 1310720 | tf_op jit(solution)/shard_map/all_gather | solution.py:14
  123.5 47.1 %copy-start.10 = (pred[256,256]{1,0:T(8,128)(4,1)S(1)}, pred[256,256]{1,0:T(8,128)(4,1)}, u32[]{:S(2)}) copy-start(pred[256,256]{1,0:T(8,128)(4,1)} %copy.24) | copy-start | bytes 196612
  123.5 47.1 %copy-start.18 = (pred[256,256]{1,0:T(8,128)(4,1)S(1)}, pred[256,256]{1,0:T(8,128)(4,1)}, u32[]{:S(2)}) copy-start(pred[256,256]{1,0:T(8,128)(4,1)} %copy.29) | copy-start | bytes 196612
  172.5 2.0 copy-start.12
  176.2 1.7 copy-start.11
  179.6 1.9 copy-start.17
  183.3 1.7 copy-start.16
  186.7 1.7 copy-start.15
  190.2 1.7 copy-start.14
  193.9 1.7 copy-start.13
  197.3 1.9 copy-start
  197.3 1.9 copy-start.8
  199.0 4.2 %copy-start.5 = (f32[3,2,256,256]{3,2,1,0:T(8,128)}, f32[3,2,256,256]{3,2,1,0:T(8,128)S(1)}, u32[]{:S(2)}) copy-start(f32[3,2,256,256]{3,2,1,0:T(8,128)S(1)} %convolution_subtract_fusion) | copy-start | bytes 4718596
  200.7 1.7 copy-start.7
  204.6 0.9 copy-start.3
  206.3 63.8 %all-gather.15.cloned.1.call-start = ((), (), s32[]{:S(2)}) async-start(), calls=%async_computation.2 | async-start | bytes 1310720 | tf_op jit(solution)/shard_map/all_gather | solution.py:14
  232.4 0.7 copy-start.9
  233.8 8.0 %collective-permute-start = (f32[256,128]{0,1:T(8,128)}, f32[256,128]{0,1:T(8,128)}, u32[]{:S(2)}, u32[]{:S(2)}) collective-permute-start(f32[256,128]{0,1:T(8,128)} %get-tuple-element.215), channel_id=1, source_target_pairs={{8,0},{16,8},{24,16},{9,1},{17,9},{25,17},{10,2},{18,10},{26,18},{... | collective-permute-start | bytes 393224 | tf_op jit(solution)/shard_map/ppermute | solution.py:28
  251.1 0.9 copy-start.4
  252.7 59.5 %all-gather.17.cloned.1.call-start = ((), (), s32[]{:S(2)}) async-start(), calls=%async_computation.3 | async-start | bytes 1310720 | tf_op jit(solution)/shard_map/all_gather | solution.py:14
  278.1 7.7 %collective-permute-start.1 = (f32[256,128]{0,1:T(8,128)S(1)}, f32[256,128]{0,1:T(8,128)S(1)}, u32[]{:S(2)}, u32[]{:S(2)}) collective-permute-start(f32[256,128]{0,1:T(8,128)S(1)} %get-tuple-element.213), channel_id=1, source_target_pairs={{8,0},{16,8},{24,16},{9,1},{17,9},{25,17},{10,2},{18,10},{26,18},{... | collective-permute-start | bytes 393224 | tf_op jit(solution)/shard_map/ppermute | solution.py:28
  293.2 0.9 copy-start.1
  312.2 2.1 copy-start.6
  313.8 1.1 copy-start.2
  315.6 6.3 %collective-permute-start.2 = (f32[256,128]{0,1:T(8,128)S(1)}, f32[256,128]{0,1:T(8,128)S(1)}, u32[]{:S(2)}, u32[]{:S(2)}) collective-permute-start(f32[256,128]{0,1:T(8,128)S(1)} %get-tuple-element.211), channel_id=1, source_target_pairs={{8,0},{16,8},{24,16},{9,1},{17,9},{25,17},{10,2},{18,10},{26,18},{... | collective-permute-start | bytes 393224 | tf_op jit(solution)/shard_map/ppermute | solution.py:28
Sparse Core Ops, SparseCore 0:
  9.5 60.3 all-gather.10
  206.4 17.5 all-gather.12
  252.8 17.1 all-gather.14
  295.0 17.1 all-gather.16
where the time goes:
time: 336 us; the launch traced here: 329 us
  local copies, waits for them, and re-layouts  129 us (38%)
  waiting for transfers between devices  90.5 us (27%)
  matrix products  60 us (18%)
  blocking collectives  23.5 us (7%)
  between operations  14.1 us (4%)
  starting transfers between devices  6.32 us (2%)
  other arithmetic  5.77 us (2%)
    all_gather x1, waiting for transfers between devices, shards(): gathered = lax.all_gather(householder, 'col', axis=3, tiled=True)  52.3 us
    dot_general x34, matrix products, product(): jnp.dot(left, right, precision=PRECISE, preferred_element_type=jnp.float32)  49.2 us
    add x1, local copies, waits for them, and re-layouts, block_inverse(): jnp.triu(gram_matrix, 1) + jnp.diag(jnp.diagonal(gram_matrix) * 0.5)  44.3 us
    dot_general x1, local copies, waits for them, and re-layouts, inner_product(): lax.dot_general(left, right, (((0,), (0,)), ((), ())), precision=PRECISE,...  43.8 us
    all_gather x3, blocking collectives, prefix_2(): gathered = jax.tree.map(lambda a: lax.all_gather(a, axis), part)  23.5 us
    all_gather x3, waiting for transfers between devices, prefix_2(): gathered = jax.tree.map(lambda a: lax.all_gather(a, axis), part)  21.6 us
    ppermute x3, waiting for transfers between devices, shifted(): lax.ppermute(value, axis, [(source, source + steps) for source in range(i...  15.8 us
    while x6, local copies, waits for them, and re-layouts, prefix_2(): return lax.fori_loop(0, place, one, state)  11.1 us
  transfers between devices with their start and end apart: 7, of which 7 were waited for; matrix products, arithmetic and copies ran while one was open for 5% of the time, Pallas kernels for 0%

commit v1 on v0

v1 whole, which is shorter than its diff:
```python
import functools
import jax
import jax.numpy as jnp
from jax import lax
from jax.experimental import pallas as pl
from jax.experimental.pallas import tpu as pltpu
from jax.sharding import PartitionSpec as P

MESH = pl.DeviceIdType.MESH
F32, BF16 = jnp.float32, jnp.bfloat16


def dot(a, b):
    return jnp.dot(a, b, preferred_element_type=F32)


def dot_nt(a, b):
    return lax.dot_general(a, b, (((1,), (1,)), ((), ())), preferred_element_type=F32)


def split(x):
    high = x.astype(BF16)
    return high, (x - high.astype(F32)).astype(BF16)


def left_pair(x):
    return jnp.concatenate(split(x), axis=1)


def right_pair(x):
    row = jnp.concatenate(split(x), axis=1)
    return jnp.concatenate([row, row], axis=0)


def fold(left, right):
    both = dot(left, right)
    half = both.shape[1] // 2
    return both[:, :half] + both[:, half:]


def kernel(outer, inner, rows_n, y_ref, vt_ref, o_ref, vt_all, qh, ql, mid, low, tx_up, tx_dn,
           rx_dn, rx_up, oa_send, oa_recv, ib_send, ib_recv, up_send, up_recv, dn_send, dn_recv):
    sweeps, per, share, block = vt_ref.shape
    refl = share * outer * inner
    half = refl // 2
    d = lax.axis_index("row")
    c = lax.axis_index("col")
    zc, yc = lax.div(c, inner), lax.rem(c, inner)

    def z_at(step):
        return lax.rem(zc + step, outer)

    def y_at(step):
        return lax.rem(yc + step, inner)

    def place(s, j, z, y):
        start = pl.multiple_of((z * inner + y) * share, share)
        return vt_all.at[s, j, pl.ds(start, share)]

    barrier = pltpu.get_barrier_semaphore()
    for step in range(1, outer):
        pl.semaphore_signal(barrier, inc=1, device_id={"col": z_at(step) * inner + yc}, device_id_type=MESH)
    for step in range(1, inner):
        pl.semaphore_signal(barrier, inc=1, device_id={"col": zc * inner + y_at(step)}, device_id_type=MESH)

    @pl.when(d > 0)
    def _():
        pl.semaphore_signal(barrier, inc=1, device_id={"row": d - 1}, device_id_type=MESH)

    @pl.when(d < rows_n - 1)
    def _():
        pl.semaphore_signal(barrier, inc=1, device_id={"row": d + 1}, device_id_type=MESH)

    greeted = (outer - 1) + (inner - 1)
    pl.semaphore_wait(barrier, greeted + jnp.where(d > 0, 1, 0) + jnp.where(d < rows_n - 1, 1, 0))

    def used(j):
        return jnp.logical_or(d > 0, j > 0)

    def outer_copy(s, j, step):
        return pltpu.make_async_remote_copy(
            src_ref=vt_ref.at[s, j], dst_ref=place(s, j, zc, yc),
            send_sem=oa_send.at[s, j, step - 1], recv_sem=oa_recv.at[s, j, zc],
            device_id={"col": z_at(step) * inner + yc}, device_id_type=MESH)

    def outer_arrival(s, j, step):
        z = z_at(step)
        return pltpu.make_async_remote_copy(
            src_ref=vt_ref.at[s, j], dst_ref=place(s, j, z, yc),
            send_sem=oa_send.at[s, j, step - 1], recv_sem=oa_recv.at[s, j, z],
            device_id={"col": z * inner + yc}, device_id_type=MESH)

    def inner_copy(s, j, step, hop):
        z = z_at(step)
        source = vt_ref.at[s, j] if step == 0 else place(s, j, z, yc)
        return pltpu.make_async_remote_copy(
            src_ref=source, dst_ref=place(s, j, z, yc),
            send_sem=ib_send.at[s, j, step, hop - 1], recv_sem=ib_recv.at[s, j, z, yc],
            device_id={"col": zc * inner + y_at(hop)}, device_id_type=MESH)

    def inner_arrival(s, j, step, hop):
        z, y = z_at(step), y_at(hop)
        return pltpu.make_async_remote_copy(
            src_ref=vt_ref.at[s, j], dst_ref=place(s, j, z, y),
            send_sem=ib_send.at[s, j, step, hop - 1], recv_sem=ib_recv.at[s, j, z, y],
            device_id={"col": zc * inner + y}, device_id_type=MESH)

    def up_copy(s):
        return pltpu.make_async_remote_copy(
            src_ref=tx_up.at[s], dst_ref=rx_up.at[s], send_sem=up_send.at[s], recv_sem=up_recv.at[s],
            device_id={"row": lax.max(d - 1, 0)}, device_id_type=MESH)

    def dn_copy(s):
        return pltpu.make_async_remote_copy(
            src_ref=tx_dn.at[s], dst_ref=rx_dn.at[s], send_sem=dn_send.at[s], recv_sem=dn_recv.at[s],
            device_id={"row": lax.min(d + 1, rows_n - 1)}, device_id_type=MESH)

    def own_inner(s):
        for j in range(per):
            @pl.when(used(j))
            def _():
                for hop in range(1, inner):
                    inner_copy(s, j, 0, hop).start()

    def forward(s, j, step, more=True):
        @pl.when(jnp.logical_and(used(j), more))
        def _():
            outer_arrival(s, j, step).wait_recv()
            for hop in range(1, inner):
                inner_copy(s, j, step, hop).start()

    for s in range(sweeps):
        for j in range(per):
            @pl.when(used(j))
            def _():
                for step in range(1, outer):
                    outer_copy(s, j, step).start()
        if s < 2:
            own_inner(s)

    for s in range(sweeps):
        for j in range(per):
            place(s, j, zc, yc)[...] = vt_ref[s, j]
    mid[...] = y_ref[:refl]
    low[...] = y_ref[refl:]

    for step in range(1, outer):
        for j in range(per):
            forward(0, j, step)

    rows_i = lax.broadcasted_iota(jnp.int32, (half, half), 0)
    cols_i = lax.broadcasted_iota(jnp.int32, (half, half), 1)
    on_diagonal = rows_i == cols_i
    above = rows_i < cols_i

    def prepare(s, points):
        points = list(points)

        def point():
            if points:
                points.pop(0)()

        vs, chains, corners = [], [], []
        for j in range(per):
            slot = jnp.where(d > 0, j, per - 1) if j == 0 else j
            vt = vt_all[s, slot]
            vh, vl = split(vt)
            vs.append((slot, vh, vl))
            top = dot_nt(vh[:half], vh) + dot_nt(vh[:half], vl) + dot_nt(vl[:half], vh)
            end = dot_nt(vh[half:], vh[half:]) + dot_nt(vh[half:], vl[half:]) + dot_nt(vl[half:], vh[half:])
            corners.append(top[:, half:])
            for gram in (top[:, :half], end):
                on = jnp.where(on_diagonal, gram, 0.0) * 0.5
                by_row = 1.0 / jnp.sum(on, axis=1, keepdims=True)
                by_col = 1.0 / jnp.sum(on, axis=0, keepdims=True)
                pairs = jnp.where(above & (rows_i // 2 == cols_i // 2), gram, 0.0)
                inverse = jnp.where(on_diagonal, by_row, 0.0) - by_row * pairs * by_col
                chains.append((gram, inverse))
        point()
        size = 2
        while size < half:
            joined = above & (rows_i // (2 * size) == cols_i // (2 * size)) & (rows_i // size != cols_i // size)
            first = [fold(left_pair(inv), right_pair(jnp.where(joined, gram, 0.0))) for gram, inv in chains]
            chains = [(gram, inv - fold(left_pair(f), right_pair(inv))) for (gram, inv), f in zip(chains, first)]
            size *= 2
            point()
        for j in range(per):
            slot, vh, vl = vs[j]
            p1, p2 = chains[2 * j][1], chains[2 * j + 1][1]
            corner = -fold(left_pair(fold(left_pair(p1), right_pair(corners[j]))), right_pair(p2))
            v = vt_all[s, slot].T
            v1, v2 = left_pair(v[:, :half]), left_pair(v[:, half:])
            a = jnp.concatenate(
                [fold(v1, right_pair(p1)), fold(v1, right_pair(corner)) + fold(v2, right_pair(p2))], axis=1)
            ah, al = split(a)
            for base in range(0, block, refl):
                ahb, alb = ah[base:base + refl], al[base:base + refl]
                q_rows = lax.broadcasted_iota(jnp.int32, (refl, block), 0) + base
                q_cols = lax.broadcasted_iota(jnp.int32, (refl, block), 1)
                unit = jnp.where(q_rows == q_cols, 1.0, 0.0)
                q = unit - (dot(ahb, vh) + dot(ahb, vl) + dot(alb, vh))
                hi, lo = split(q)
                qh[j, base:base + refl] = hi
                ql[j, base:base + refl] = lo
        while points:
            point()

    def apply_half(j, base, y_pair, y_high):
        both = dot(qh[j, base:base + refl], y_pair)
        cols = y_high.shape[1]
        return both[:, :cols] + both[:, cols:] + dot(ql[j, base:base + refl], y_high)

    def sweep(s, carry):
        nxt = lax.min(s + 1, sweeps - 1)
        more = s + 1 < sweeps

        @pl.when(s + 2 < sweeps)
        def _():
            own_inner(lax.min(s + 2, sweeps - 1))

        for j in range(per):
            @pl.when(used(j))
            def _():
                for step in range(outer):
                    for hop in range(1, inner):
                        inner_arrival(s, j, step, hop).wait_recv()

        prepare(s, [functools.partial(forward, nxt, j, step, more) for step in range(1, outer) for j in range(per)])

        @pl.when(d > 0)
        def _():
            dn_copy(s).wait_recv()
            y = jnp.concatenate([rx_dn[s], mid[...]], axis=0)
            high, rest = split(y)
            y_pair = jnp.concatenate([high, rest], axis=1)
            tx_up[s] = apply_half(0, 0, y_pair, high)
            up_copy(s).start()
            mid[...] = apply_half(0, refl, y_pair, high)

        @pl.when(jnp.logical_and(d < rows_n - 1, s > 0))
        def _():
            before = lax.max(s - 1, 0)
            up_copy(before).wait_recv()
            low[...] = rx_up[before]

        y = jnp.concatenate([mid[...], low[...]], axis=0)
        high, rest = split(y)
        y_pair = jnp.concatenate([high, rest], axis=1)
        new_low = apply_half(1, refl, y_pair, high)
        low[...] = new_low
        tx_dn[s] = new_low

        @pl.when(d < rows_n - 1)
        def _():
            dn_copy(s).start()

        mid[...] = apply_half(1, 0, y_pair, high)
        return carry

    lax.fori_loop(0, sweeps, sweep, 0)

    o_ref[:refl] = mid[...]

    @pl.when(d < rows_n - 1)
    def _():
        up_copy(sweeps - 1).wait_recv()
        o_ref[refl:] = rx_up[sweeps - 1]

    @pl.when(d == rows_n - 1)
    def _():
        o_ref[refl:] = low[...]

    for s in range(sweeps):
        for j in range(per):
            @pl.when(used(j))
            def _():
                for step in range(1, outer):
                    outer_copy(s, j, step).wait_send()
                for step in range(outer):
                    for hop in range(1, inner):
                        inner_copy(s, j, step, hop).wait_send()

        @pl.when(d > 0)
        def _():
            up_copy(s).wait_send()

        @pl.when(d < rows_n - 1)
        def _():
            dn_copy(s).wait_send()


def solution(mesh):
    rows_n, cols_n = mesh.shape["row"], mesh.shape["col"]
    inner = 1
    while (2 * inner) * (2 * inner) <= cols_n and cols_n % (2 * inner) == 0:
        inner *= 2
    outer = cols_n // inner

    def shards(eigenvectors, householder):
        vt = jnp.swapaxes(householder, 2, 3)
        sweeps, per, share, block = vt.shape
        rows, cols = eigenvectors.shape
        refl = share * cols_n
        dma = pltpu.SemaphoreType.DMA
        vmem = pl.BlockSpec(memory_space=pltpu.VMEM)
        return pl.pallas_call(
            functools.partial(kernel, outer, inner, rows_n),
            out_shape=jax.ShapeDtypeStruct((rows, cols), F32),
            in_specs=[vmem] * 2,
            out_specs=vmem,
            scratch_shapes=[
                pltpu.VMEM((sweeps, per, refl, block), F32),
                pltpu.VMEM((per, block, block), BF16),
                pltpu.VMEM((per, block, block), BF16),
                pltpu.VMEM((refl, cols), F32),
                pltpu.VMEM((refl, cols), F32),
                pltpu.VMEM((sweeps, refl, cols), F32),
                pltpu.VMEM((sweeps, refl, cols), F32),
                pltpu.VMEM((sweeps, refl, cols), F32),
                pltpu.VMEM((sweeps, refl, cols), F32),
                dma((sweeps, per, outer)),
                dma((sweeps, per, outer)),
                dma((sweeps, per, outer, inner)),
                dma((sweeps, per, outer, inner)),
                dma((sweeps,)), dma((sweeps,)), dma((sweeps,)), dma((sweeps,)),
            ],
            compiler_params=pltpu.CompilerParams(
                collective_id=0, has_side_effects=True, vmem_limit_bytes=60 * 2**20),
        )(eigenvectors, vt)

    return jax.shard_map(
        shards, mesh=mesh, in_specs=(P("row", "col"), P(None, "row", None, "col")),
        out_specs=P("row", "col"), check_vma=False)
```

time: 336 us -> 66.4 us (0.20)
  the two profiles are of different devices: /device:TPU:1 before, /device:TPU:13 now
where the time goes in v1:
time: 66.4 us; the launch traced here: 66.3 us
  Pallas kernels  64.6 us (97%)
  local copies, waits for them, and re-layouts  1.67 us (3%)
    pallas_call x1, Pallas kernels, shards(): pl.pallas_call(functools.partial(kernel, outer, inner, rows_n), out_shape...  64.6 us
    unnamed x1, local copies, waits for them, and re-layouts  1.67 us

profile of v1, /device:TPU:13, one launch (start us, length us, event | category | flops | bytes accessed | tf_op | source)
XLA Modules:
  0.0 66.3 jit_solution(18369521610156076804)
XLA Ops:
  0.0 64.6 %shard_map.28 = f32[512,128]{1,0:T(8,128)} custom-call(f32[512,128]{1,0:T(8,128)} %y_ref.1, f32[3,2,32,512]{3,2,1,0:T(8,128)} %bitcast.1), custom_call_target="tpu_custom_call" | custom-call | tf_op jit(solution)/shard_map/pallas_call | solution.py:306
  64.6 1.7 %copy.4 = f32[512,128]{1,0:T(8,128)} copy(f32[512,128]{1,0:T(8,128)} %shard_map.28) | data formatting | bytes 524288

commit v2 on v1

--- a/solution.py
+++ b/solution.py
@@ -77,32 +77,32 @@
     def used(j):
         return jnp.logical_or(d > 0, j > 0)
 
-    def outer_copy(s, j, step):
-        return pltpu.make_async_remote_copy(
-            src_ref=vt_ref.at[s, j], dst_ref=place(s, j, zc, yc),
-            send_sem=oa_send.at[s, j, step - 1], recv_sem=oa_recv.at[s, j, zc],
-            device_id={"col": z_at(step) * inner + yc}, device_id_type=MESH)
-
-    def outer_arrival(s, j, step):
-        z = z_at(step)
-        return pltpu.make_async_remote_copy(
-            src_ref=vt_ref.at[s, j], dst_ref=place(s, j, z, yc),
-            send_sem=oa_send.at[s, j, step - 1], recv_sem=oa_recv.at[s, j, z],
-            device_id={"col": z * inner + yc}, device_id_type=MESH)
-
-    def inner_copy(s, j, step, hop):
-        z = z_at(step)
-        source = vt_ref.at[s, j] if step == 0 else place(s, j, z, yc)
-        return pltpu.make_async_remote_copy(
-            src_ref=source, dst_ref=place(s, j, z, yc),
-            send_sem=ib_send.at[s, j, step, hop - 1], recv_sem=ib_recv.at[s, j, z, yc],
+    def outer_copy(s, j, z, side, own=False):
+        there = lax.min(zc + 1, outer - 1) if side == 0 else lax.max(zc - 1, 0)
+        return pltpu.make_async_remote_copy(
+            src_ref=vt_ref.at[s, j] if own else place(s, j, z, yc), dst_ref=place(s, j, z, yc),
+            send_sem=oa_send.at[s, j, side, z], recv_sem=oa_recv.at[s, j, z],
+            device_id={"col": there * inner + yc}, device_id_type=MESH)
+
+    def goes_on(side):
+        return zc < outer - 1 if side == 0 else zc > 0
+
+    def piece_at(side, distance):
+        if side == 0:
+            return lax.max(zc - distance, 0), zc - distance >= 0
+        return lax.min(zc + distance, outer - 1), zc + distance < outer
+
+    def inner_copy(s, j, z, hop, own=False):
+        return pltpu.make_async_remote_copy(
+            src_ref=vt_ref.at[s, j] if own else place(s, j, z, yc), dst_ref=place(s, j, z, yc),
+            send_sem=ib_send.at[s, j, z, hop - 1], recv_sem=ib_recv.at[s, j, z, yc],
             device_id={"col": zc * inner + y_at(hop)}, device_id_type=MESH)
 
-    def inner_arrival(s, j, step, hop):
-        z, y = z_at(step), y_at(hop)
+    def inner_arrival(s, j, z, hop):
+        y = y_at(hop)
         return pltpu.make_async_remote_copy(
             src_ref=vt_ref.at[s, j], dst_ref=place(s, j, z, y),
-            send_sem=ib_send.at[s, j, step, hop - 1], recv_sem=ib_recv.at[s, j, z, y],
+            send_sem=ib_send.at[s, j, z, hop - 1], recv_sem=ib_recv.at[s, j, z, y],
             device_id={"col": zc * inner + y}, device_id_type=MESH)
 
     def up_copy(s):
@@ -120,21 +120,29 @@
             @pl.when(used(j))
             def _():
                 for hop in range(1, inner):
-                    inner_copy(s, j, 0, hop).start()
-
-    def forward(s, j, step, more=True):
-        @pl.when(jnp.logical_and(used(j), more))
-        def _():
-            outer_arrival(s, j, step).wait_recv()
-            for hop in range(1, inner):
-                inner_copy(s, j, step, hop).start()
+                    inner_copy(s, j, zc, hop, True).start()
+
+    def forward(s, j, distance, more=True):
+        for side in (0, 1):
+            z, there = piece_at(side, distance)
+
+            @pl.when(jnp.logical_and(jnp.logical_and(used(j), there), more))
+            def _():
+                outer_copy(s, j, z, side).wait_recv()
+
+                @pl.when(goes_on(side))
+                def _():
+                    outer_copy(s, j, z, side).start()
+
+                for hop in range(1, inner):
+                    inner_copy(s, j, z, hop).start()
 
     for s in range(sweeps):
         for j in range(per):
-            @pl.when(used(j))
-            def _():
-                for step in range(1, outer):
-                    outer_copy(s, j, step).start()
+            for side in (0, 1):
+                @pl.when(jnp.logical_and(used(j), goes_on(side)))
+                def _():
+                    outer_copy(s, j, zc, side, True).start()
         if s < 2:
             own_inner(s)
 
@@ -144,9 +152,13 @@
     mid[...] = y_ref[:refl]
     low[...] = y_ref[refl:]
 
-    for step in range(1, outer):
-        for j in range(per):
-            forward(0, j, step)
+    pieces = [(j, distance) for j in range(per) for distance in range(1, outer)]
+    ahead = min(2, len(pieces))
+    for j, step in pieces:
+        forward(0, j, step)
+    if sweeps > 1:
+        for j, step in pieces[:ahead]:
+            forward(1, j, step)
 
     rows_i = lax.broadcasted_iota(jnp.int32, (half, half), 0)
     cols_i = lax.broadcasted_iota(jnp.int32, (half, half), 1)
@@ -211,21 +223,31 @@
         return both[:, :cols] + both[:, cols:] + dot(ql[j, base:base + refl], y_high)
 
     def sweep(s, carry):
-        nxt = lax.min(s + 1, sweeps - 1)
-        more = s + 1 < sweeps
-
-        @pl.when(s + 2 < sweeps)
-        def _():
-            own_inner(lax.min(s + 2, sweeps - 1))
+        nxt, later = lax.min(s + 1, sweeps - 1), lax.min(s + 2, sweeps - 1)
+        more, still = s + 1 < sweeps, s + 2 < sweeps
+
+        @pl.when(still)
+        def _():
+            own_inner(later)
 
         for j in range(per):
             @pl.when(used(j))
             def _():
-                for step in range(outer):
+                for z in range(outer):
                     for hop in range(1, inner):
-                        inner_arrival(s, j, step, hop).wait_recv()
-
-        prepare(s, [functools.partial(forward, nxt, j, step, more) for step in range(1, outer) for j in range(per)])
+                        inner_arrival(s, j, z, hop).wait_recv()
+
+        def early(i):
+            return 2 * d >= i
+
+        points = []
+        for i, (j, step) in list(enumerate(pieces))[ahead:]:
+            waits = jnp.logical_and(more, jnp.logical_not(jnp.logical_and(s > 0, early(i))))
+            points.append(functools.partial(forward, nxt, j, step, waits))
+        points += [functools.partial(forward, later, j, step, still) for j, step in pieces[:ahead]]
+        prepare(s, points)
+        for i, (j, step) in list(enumerate(pieces))[ahead:]:
+            forward(later, j, step, jnp.logical_and(still, early(i)))
 
         @pl.when(d > 0)
         def _():
@@ -274,11 +296,16 @@
         for j in range(per):
             @pl.when(used(j))
             def _():
-                for step in range(1, outer):
-                    outer_copy(s, j, step).wait_send()
-                for step in range(outer):
+                for z in range(outer):
                     for hop in range(1, inner):
-                        inner_copy(s, j, step, hop).wait_send()
+                        inner_copy(s, j, z, hop).wait_send()
+                for side in (0, 1):
+                    for distance in range(outer):
+                        z, there = piece_at(side, distance)
+
+                        @pl.when(jnp.logical_and(there, goes_on(side)))
+                        def _():
+                            outer_copy(s, j, z, side).wait_send()
 
         @pl.when(d > 0)
         def _():
@@ -318,7 +345,7 @@
                 pltpu.VMEM((sweeps, refl, cols), F32),
                 pltpu.VMEM((sweeps, refl, cols), F32),
                 pltpu.VMEM((sweeps, refl, cols), F32),
-                dma((sweeps, per, outer)),
+                dma((sweeps, per, 2, outer)),
                 dma((sweeps, per, outer)),
                 dma((sweeps, per, outer, inner)),
                 dma((sweeps, per, outer, inner)),

time: 66.4 us -> 63.6 us (0.958)
  the two profiles are of different devices: /device:TPU:13 before, /device:TPU:1 now
where the time goes in v2:
time: 63.6 us; the launch traced here: 63.5 us
  Pallas kernels  61.8 us (97%)
  local copies, waits for them, and re-layouts  1.67 us (3%)
    pallas_call x1, Pallas kernels, shards(): pl.pallas_call(functools.partial(kernel, outer, inner, rows_n), out_shape...  61.8 us
    unnamed x1, local copies, waits for them, and re-layouts  1.67 us

profile of v2, /device:TPU:1, one launch (start us, length us, event | category | flops | bytes accessed | tf_op | source)
XLA Modules:
  0.0 63.5 jit_solution(5079151265023729888)
XLA Ops:
  0.0 61.8 %shard_map.28 = f32[512,128]{1,0:T(8,128)} custom-call(f32[512,128]{1,0:T(8,128)} %y_ref.1, f32[3,2,32,512]{3,2,1,0:T(8,128)} %bitcast.1), custom_call_target="tpu_custom_call" | custom-call | tf_op jit(solution)/shard_map/pallas_call | solution.py:333
  61.8 1.7 %copy.4 = f32[512,128]{1,0:T(8,128)} copy(f32[512,128]{1,0:T(8,128)} %shard_map.28) | data formatting | bytes 524288

commit v3 on v2

--- a/solution.py
+++ b/solution.py
@@ -137,14 +137,16 @@
                 for hop in range(1, inner):
                     inner_copy(s, j, z, hop).start()
 
-    for s in range(sweeps):
+    def own_outer(s):
         for j in range(per):
             for side in (0, 1):
                 @pl.when(jnp.logical_and(used(j), goes_on(side)))
                 def _():
                     outer_copy(s, j, zc, side, True).start()
-        if s < 2:
-            own_inner(s)
+
+    for s in range(min(sweeps, 2)):
+        own_outer(s)
+        own_inner(s)
 
     for s in range(sweeps):
         for j in range(per):
@@ -228,6 +230,7 @@
 
         @pl.when(still)
         def _():
+            own_outer(later)
             own_inner(later)
 
         for j in range(per):

time: 63.6 us -> 61.3 us (0.964)
  Pallas kernels: 61.8 us -> 59.4 us
    pallas_call x1, Pallas kernels: 61.8 us -> 59.4 us  [shards(): pl.pallas_call(functools.partial(kernel, outer, inner, rows_n), out_shape...]
where the time goes in v3:
time: 61.3 us; the launch traced here: 61.1 us
  Pallas kernels  59.4 us (97%)
  local copies, waits for them, and re-layouts  1.67 us (3%)
    pallas_call x1, Pallas kernels, shards(): pl.pallas_call(functools.partial(kernel, outer, inner, rows_n), out_shape...  59.4 us
    unnamed x1, local copies, waits for them, and re-layouts  1.67 us

profile of v3, /device:TPU:1, one launch (start us, length us, event | category | flops | bytes accessed | tf_op | source)
XLA Modules:
  0.0 61.1 jit_solution(215890664378704183)
XLA Ops:
  0.0 59.4 %shard_map.28 = f32[512,128]{1,0:T(8,128)} custom-call(f32[512,128]{1,0:T(8,128)} %y_ref.1, f32[3,2,32,512]{3,2,1,0:T(8,128)} %bitcast.1), custom_call_target="tpu_custom_call" | custom-call | tf_op jit(solution)/shard_map/pallas_call | solution.py:336
  59.4 1.7 %copy.4 = f32[512,128]{1,0:T(8,128)} copy(f32[512,128]{1,0:T(8,128)} %shard_map.28) | data formatting | bytes 524288
